TPU v7x, 32 devices: a whole 2x2x4 slice. The times are simulated.
32 devices in a mesh: dp: 8 (over z, y), seq: 4 (over x, core).
Axes of the slice: x: 2, y: 2, z: 4, core: 2. Of those that a mesh axis runs over, the one named last changes fastest.
Arguments:
- inputs: bfloat16 [16, 1024, 768], P('dp', 'seq'), may hold values from -6 to 6
- lengths: int32 [16], P('dp'), may hold values from 512 to 1024, as said below
- query_weight: bfloat16 [768, 768], P('dp'), may hold values from -0.3125 to 0.3125
- key_weight: bfloat16 [768, 768], P('dp'), may hold values from -0.3125 to 0.3125
- value_weight: bfloat16 [768, 768], P('dp'), may hold values from -0.21875 to 0.21875
- output_weight: bfloat16 [768, 768], P('dp'), may hold values from -0.625 to 0.625
- up_weight: bfloat16 [768, 3072], P('dp'), may hold values from -0.21875 to 0.21875
- down_weight: bfloat16 [3072, 768], P('dp'), may hold values from -0.15625 to 0.15625
- query_bias: bfloat16 [768], P('dp'), may hold values from -3 to 3
- value_bias: bfloat16 [768], P('dp'), may hold values from -3 to 3
- output_bias: bfloat16 [768], P('dp'), may hold values from -3 to 3
- up_bias: bfloat16 [3072], P('dp'), may hold values from -3 to 3
- down_bias: bfloat16 [768], P('dp'), may hold values from -3 to 3
- first_gain: bfloat16 [768], P('dp'), may hold values from 0.5 to 1.5
- first_shift: bfloat16 [768], P('dp'), may hold values from -2 to 2
- second_gain: bfloat16 [768], P('dp'), may hold values from 0.5 to 1.5
- second_shift: bfloat16 [768], P('dp'), may hold values from -2 to 2
- cotangent: bfloat16 [16, 1024, 768], P('dp', 'seq'), may hold values from -6 to 6
Outputs:
- layer_out: bfloat16 [16, 1024, 768], P('dp', 'seq')
- input_grad: bfloat16 [16, 1024, 768], P('dp', 'seq')
- query_weight_grad: float32 [768, 768], P('dp')
- key_weight_grad: float32 [768, 768], P('dp')
- value_weight_grad: float32 [768, 768], P('dp')
- output_weight_grad: float32 [768, 768], P('dp')
- up_weight_grad: float32 [768, 3072], P('dp')
- down_weight_grad: float32 [3072, 768], P('dp')
- query_bias_grad: float32 [768], P('dp')
- value_bias_grad: float32 [768], P('dp')
- output_bias_grad: float32 [768], P('dp')
- up_bias_grad: float32 [3072], P('dp')
- down_bias_grad: float32 [768], P('dp')
- first_gain_grad: float32 [768], P('dp')
- first_shift_grad: float32 [768], P('dp')
- second_gain_grad: float32 [768], P('dp')
- second_shift_grad: float32 [768], P('dp')
Inputs may be any that keep to these rules, and one draw needn't show every extreme that they name: `lengths`: the number of real tokens of each sequence; its later positions up to 1024 are padding.
All inputs are finite; a program needn't handle non-finite values.
Results may differ from a plain program's by a relative error of at most 0.015.
Values may be sent and summed in bfloat16 or wider, within the bound.
A program may use at most 192 MiB of HBM per device.

v0:
```python
import jax
import jax.numpy as jnp
from jax import lax
from jax.sharding import PartitionSpec as P

HEAD_DIM = 64
eps_norm = 1e-05
masked_score = -1000000000.0


def layer_norm(hidden, gain_vec, shift_vec):
    row_mean = jnp.mean(hidden, axis=-1, keepdims=True)
    centred = hidden - row_mean
    row_var = jnp.mean(centred * centred, axis=-1, keepdims=True)
    return centred * lax.rsqrt(row_var + eps_norm) * gain_vec + shift_vec


def gelu_exact(pre_act):
    return jax.nn.gelu(pre_act, approximate=False)


def matmul_plain(first_op, second_op):
    return jnp.dot(first_op, second_op, preferred_element_type=jnp.float32)


def inner_rows(first_op, second_op):
    return lax.dot_general(
        first_op, second_op, (((0,), (0,)), ((), ())), preferred_element_type=jnp.float32
    )


def times_transposed(first_op, second_op):
    return lax.dot_general(
        first_op, second_op, (((1,), (1,)), ((), ())), preferred_element_type=jnp.float32
    )


def column_sums(grad_rows):
    return jnp.sum(grad_rows.astype(jnp.float32), axis=0)


def local(
    inputs,
    lengths,
    query_weight,
    key_weight,
    value_weight,
    output_weight,
    up_weight,
    down_weight,
    query_bias,
    value_bias,
    output_bias,
    up_bias,
    down_bias,
    first_gain,
    first_shift,
    second_gain,
    second_shift,
    cotangent,
):
    gathered = (
        lax.all_gather(query_weight, "dp", axis=0, tiled=True),
        lax.all_gather(key_weight, "dp", axis=0, tiled=True),
        lax.all_gather(value_weight, "dp", axis=0, tiled=True),
        lax.all_gather(output_weight, "dp", axis=0, tiled=True),
        lax.all_gather(up_weight, "dp", axis=0, tiled=True),
        lax.all_gather(down_weight, "dp", axis=0, tiled=True),
        lax.all_gather(query_bias, "dp", axis=0, tiled=True),
        lax.all_gather(value_bias, "dp", axis=0, tiled=True),
        lax.all_gather(output_bias, "dp", axis=0, tiled=True),
        lax.all_gather(up_bias, "dp", axis=0, tiled=True),
        lax.all_gather(down_bias, "dp", axis=0, tiled=True),
        lax.all_gather(first_gain, "dp", axis=0, tiled=True),
        lax.all_gather(first_shift, "dp", axis=0, tiled=True),
        lax.all_gather(second_gain, "dp", axis=0, tiled=True),
        lax.all_gather(second_shift, "dp", axis=0, tiled=True),
    )
    full_query, full_key, full_value, full_output, full_up, full_down = gathered[0:6]
    bias_query = gathered[6].astype(jnp.float32)
    bias_value = gathered[7].astype(jnp.float32)
    bias_output = gathered[8].astype(jnp.float32)
    bias_up = gathered[9].astype(jnp.float32)
    bias_down = gathered[10].astype(jnp.float32)
    gain_first = gathered[11].astype(jnp.float32)
    shift_first = gathered[12].astype(jnp.float32)
    gain_second = gathered[13].astype(jnp.float32)
    shift_second = gathered[14].astype(jnp.float32)
    group_count, local_len, model_width = inputs.shape
    row_count = group_count * local_len
    flat_in = inputs.reshape(row_count, model_width)
    queries = (matmul_plain(flat_in, full_query) + bias_query).astype(jnp.bfloat16)
    key_rows = matmul_plain(flat_in, full_key).astype(jnp.bfloat16)
    value_rows = (matmul_plain(flat_in, full_value) + bias_value).astype(jnp.bfloat16)
    stacked = jnp.stack([queries, key_rows, value_rows]).reshape(
        3, group_count, local_len, model_width
    )
    head_layout = lax.all_to_all(stacked, "seq", split_axis=3, concat_axis=2, tiled=True)
    seq_len = head_layout.shape[2]
    head_width = head_layout.shape[3]
    local_heads = head_width // HEAD_DIM
    block_rows = min(512, seq_len)
    block_count = seq_len // block_rows
    score_scale = HEAD_DIM ** (-0.5)

    def attend_forward(operands):
        seq_queries, seq_keys, seq_values, length = operands
        key_heads = seq_keys.reshape(seq_len, local_heads, HEAD_DIM)
        value_heads = seq_values.reshape(seq_len, local_heads, HEAD_DIM)
        key_live = jnp.arange(seq_len) < length

        def one_block(query_block):
            scores = (
                jnp.einsum(
                    "qhd,khd->hqk", query_block, key_heads, preferred_element_type=jnp.float32
                )
                * score_scale
            )
            scores = jnp.where(key_live[None, None, :], scores, masked_score)
            row_top = jnp.max(scores, axis=-1, keepdims=True)
            exponent = jnp.exp(scores - row_top)
            row_total = jnp.sum(exponent, axis=-1, keepdims=True)
            probabilities = (exponent / row_total).astype(jnp.bfloat16)
            context = jnp.einsum(
                "hqk,khd->qhd", probabilities, value_heads, preferred_element_type=jnp.float32
            )
            return (
                context.reshape(block_rows, head_width).astype(jnp.bfloat16),
                (row_top + jnp.log(row_total))[..., 0],
            )

        contexts, block_sums = lax.map(
            one_block, seq_queries.reshape(block_count, block_rows, local_heads, HEAD_DIM)
        )
        return (contexts.reshape(seq_len, head_width), block_sums)

    head_context, log_sums = lax.map(
        attend_forward, (head_layout[0], head_layout[1], head_layout[2], lengths)
    )
    context_rows = lax.all_to_all(
        head_context, "seq", split_axis=1, concat_axis=2, tiled=True
    ).reshape(row_count, model_width)
    attended = matmul_plain(context_rows, full_output) + bias_output
    first_sum = flat_in.astype(jnp.float32) + attended
    first_norm = layer_norm(first_sum, gain_first, shift_first).astype(jnp.bfloat16)
    up_pre = matmul_plain(first_norm, full_up) + bias_up
    hidden_act = gelu_exact(up_pre).astype(jnp.bfloat16)
    down_out = matmul_plain(hidden_act, full_down) + bias_down
    second_sum = first_norm.astype(jnp.float32) + down_out
    layer_out = layer_norm(second_sum, gain_second, shift_second).astype(jnp.bfloat16)
    regathered = (
        lax.all_gather(query_weight, "dp", axis=0, tiled=True),
        lax.all_gather(key_weight, "dp", axis=0, tiled=True),
        lax.all_gather(value_weight, "dp", axis=0, tiled=True),
        lax.all_gather(output_weight, "dp", axis=0, tiled=True),
        lax.all_gather(up_weight, "dp", axis=0, tiled=True),
        lax.all_gather(down_weight, "dp", axis=0, tiled=True),
        lax.all_gather(up_bias, "dp", axis=0, tiled=True),
    )
    full_query, full_key, full_value, full_output, full_up, full_down = regathered[0:6]
    bias_up = regathered[6].astype(jnp.float32)
    positions = lax.axis_index("seq") * local_len + jnp.arange(local_len)
    live_rows = (positions[None, :] < lengths[:, None]).reshape(row_count).astype(jnp.float32)
    grad_out = cotangent.reshape(row_count, model_width).astype(jnp.float32) * live_rows[:, None]
    norm_value, second_pull = jax.vjp(layer_norm, second_sum, gain_second, shift_second)
    second_sum_grad, second_gain_grad, second_shift_grad = second_pull(grad_out)
    down_grad_low = second_sum_grad.astype(jnp.bfloat16)
    down_weight_grad = inner_rows(hidden_act, down_grad_low)
    down_bias_grad = column_sums(down_grad_low)
    grad_hidden = times_transposed(down_grad_low, full_down)
    gelu_value, gelu_pull = jax.vjp(gelu_exact, up_pre)
    (up_grad_full,) = gelu_pull(grad_hidden)
    up_grad_low = up_grad_full.astype(jnp.bfloat16)
    up_weight_grad = inner_rows(first_norm, up_grad_low)
    up_bias_grad = column_sums(up_grad_low)
    first_norm_grad = second_sum_grad + times_transposed(up_grad_low, full_up)
    first_value, first_pull = jax.vjp(layer_norm, first_sum, gain_first, shift_first)
    first_sum_grad, first_gain_grad, first_shift_grad = first_pull(first_norm_grad)
    attended_low = first_sum_grad.astype(jnp.bfloat16)
    output_weight_grad = inner_rows(context_rows, attended_low)
    output_bias_grad = column_sums(attended_low)
    context_grad = times_transposed(attended_low, full_output).astype(jnp.bfloat16)
    grad_heads = lax.all_to_all(
        context_grad.reshape(group_count, local_len, model_width),
        "seq",
        split_axis=2,
        concat_axis=1,
        tiled=True,
    )

    def attend_backward(operands):
        seq_queries, seq_keys, seq_values, seq_grad, seq_sums, length = operands
        key_heads = seq_keys.reshape(seq_len, local_heads, HEAD_DIM)
        value_heads = seq_values.reshape(seq_len, local_heads, HEAD_DIM)
        key_live = jnp.arange(seq_len) < length

        def one_block(running, block_in):
            key_total, value_total = running
            query_block, grad_block, sum_block = block_in
            scores = (
                jnp.einsum(
                    "qhd,khd->hqk", query_block, key_heads, preferred_element_type=jnp.float32
                )
                * score_scale
            )
            scores = jnp.where(key_live[None, None, :], scores, masked_score)
            probabilities = jnp.exp(scores - sum_block[..., None])
            grad_probs = jnp.einsum(
                "qhd,khd->hqk", grad_block, value_heads, preferred_element_type=jnp.float32
            )
            row_delta = jnp.sum(probabilities * grad_probs, axis=-1, keepdims=True)
            grad_scores = (probabilities * (grad_probs - row_delta)).astype(jnp.bfloat16)
            query_grad = (
                jnp.einsum(
                    "hqk,khd->qhd", grad_scores, key_heads, preferred_element_type=jnp.float32
                )
                * score_scale
            )
            key_total = (
                key_total
                + jnp.einsum(
                    "hqk,qhd->khd", grad_scores, query_block, preferred_element_type=jnp.float32
                )
                * score_scale
            )
            value_total = value_total + jnp.einsum(
                "hqk,qhd->khd",
                probabilities.astype(jnp.bfloat16),
                grad_block,
                preferred_element_type=jnp.float32,
            )
            return (
                (key_total, value_total),
                query_grad.reshape(block_rows, head_width).astype(jnp.bfloat16),
            )

        zero_heads = jnp.zeros((seq_len, local_heads, HEAD_DIM), jnp.float32)
        block_shape = (block_count, block_rows, local_heads, HEAD_DIM)
        (key_total, value_total), query_grads = lax.scan(
            one_block,
            (zero_heads, zero_heads),
            (seq_queries.reshape(block_shape), seq_grad.reshape(block_shape), seq_sums),
        )
        return jnp.stack(
            [
                query_grads.reshape(seq_len, head_width),
                key_total.reshape(seq_len, head_width).astype(jnp.bfloat16),
                value_total.reshape(seq_len, head_width).astype(jnp.bfloat16),
            ]
        )

    head_grads = lax.map(
        attend_backward,
        (head_layout[0], head_layout[1], head_layout[2], grad_heads, log_sums, lengths),
    )
    row_grads = lax.all_to_all(head_grads, "seq", split_axis=2, concat_axis=3, tiled=True)
    query_grad_low = row_grads[:, 0].reshape(row_count, model_width)
    key_grad_low = row_grads[:, 1].reshape(row_count, model_width)
    value_grad_low = row_grads[:, 2].reshape(row_count, model_width)
    query_weight_grad = inner_rows(flat_in, query_grad_low)
    key_weight_grad = inner_rows(flat_in, key_grad_low)
    value_weight_grad = inner_rows(flat_in, value_grad_low)
    query_bias_grad = column_sums(query_grad_low)
    value_bias_grad = column_sums(value_grad_low)
    input_grad = (
        first_sum_grad
        + times_transposed(query_grad_low, full_query)
        + times_transposed(key_grad_low, full_key)
        + times_transposed(value_grad_low, full_value)
    ).astype(jnp.bfloat16)
    input_grad = input_grad.reshape(group_count, local_len, model_width)
    summed = (
        lax.psum_scatter(query_weight_grad, "dp", scatter_dimension=0, tiled=True),
        lax.psum_scatter(key_weight_grad, "dp", scatter_dimension=0, tiled=True),
        lax.psum_scatter(value_weight_grad, "dp", scatter_dimension=0, tiled=True),
        lax.psum_scatter(output_weight_grad, "dp", scatter_dimension=0, tiled=True),
        lax.psum_scatter(up_weight_grad, "dp", scatter_dimension=0, tiled=True),
        lax.psum_scatter(down_weight_grad, "dp", scatter_dimension=0, tiled=True),
        lax.psum_scatter(query_bias_grad, "dp", scatter_dimension=0, tiled=True),
        lax.psum_scatter(value_bias_grad, "dp", scatter_dimension=0, tiled=True),
        lax.psum_scatter(output_bias_grad, "dp", scatter_dimension=0, tiled=True),
        lax.psum_scatter(up_bias_grad, "dp", scatter_dimension=0, tiled=True),
        lax.psum_scatter(down_bias_grad, "dp", scatter_dimension=0, tiled=True),
        lax.psum_scatter(first_gain_grad, "dp", scatter_dimension=0, tiled=True),
        lax.psum_scatter(first_shift_grad, "dp", scatter_dimension=0, tiled=True),
        lax.psum_scatter(second_gain_grad, "dp", scatter_dimension=0, tiled=True),
        lax.psum_scatter(second_shift_grad, "dp", scatter_dimension=0, tiled=True),
    )
    totals = lax.psum(
        (
            summed[0],
            summed[1],
            summed[2],
            summed[3],
            summed[4],
            summed[5],
            summed[6],
            summed[7],
            summed[8],
            summed[9],
            summed[10],
            summed[11],
            summed[12],
            summed[13],
            summed[14],
        ),
        "seq",
    )
    layer_out = layer_out.reshape(group_count, local_len, model_width)
    return (
        layer_out,
        input_grad,
        totals[0],
        totals[1],
        totals[2],
        totals[3],
        totals[4],
        totals[5],
        totals[6],
        totals[7],
        totals[8],
        totals[9],
        totals[10],
        totals[11],
        totals[12],
        totals[13],
        totals[14],
    )


def solution(mesh):
    return jax.shard_map(
        local,
        mesh=mesh,
        in_specs=(
            P("dp", "seq", None),
            P("dp"),
            P("dp", None),
            P("dp", None),
            P("dp", None),
            P("dp", None),
            P("dp", None),
            P("dp", None),
            P("dp"),
            P("dp"),
            P("dp"),
            P("dp"),
            P("dp"),
            P("dp"),
            P("dp"),
            P("dp"),
            P("dp"),
            P("dp", "seq", None),
        ),
        out_specs=(
            P("dp", "seq", None),
            P("dp", "seq", None),
            P("dp", None),
            P("dp", None),
            P("dp", None),
            P("dp", None),
            P("dp", None),
            P("dp", None),
            P("dp"),
            P("dp"),
            P("dp"),
            P("dp"),
            P("dp"),
            P("dp"),
            P("dp"),
            P("dp"),
            P("dp"),
        ),
        check_vma=False,
    )
```

profile of v0, /device:TPU:0, one launch (start us, length us, event | category | flops | bytes accessed | tf_op | source)
XLA Modules:
  0.0 1238.4 jit_solution(14016261787662703552)
XLA Ops:
  19.3 39.9 %all-reduce.20 = (bf16[768]{0:T(1024)(128)(2,1)S(1)}, bf16[768]{0:T(1024)(128)(2,1)S(1)}, bf16[768]{0:T(1024)(128)(2,1)}, bf16[768]{0:T(1024)(128)(2,1)}, bf16[7...) all-reduce(bf16[768]{0:T(1024)(128)(2,1)S(1)} %dynamic-update-slice, ...), channel_id=1, replica_groups=mesh['dp'=8,'seq'=4] {'dp'}, use_global_device_ids=true, to_apply=%add.1 | all-reduce | flops 6144 | bytes 24576
  62.1 34.2 %all-gather.12.cloned.1.call-done = bf16[768,768]{1,0:T(8,128)(2,1)} async-done(((bf16[96,768]{1,0:T(8,128)(2,1)}), bf16[768,768]{1,0:T(8,128)(2,1)}) %all-gather.12.cloned.1.call-update) | async-done | bytes 1179664 | tf_op jit(solution)/shard_map/all_gather | solution.py:65
  99.0 39.3 %all-gather.10.cloned.1.call-done = bf16[768,768]{1,0:T(8,128)(2,1)} async-done(((bf16[96,768]{1,0:T(8,128)(2,1)}), bf16[768,768]{1,0:T(8,128)(2,1)}) %all-gather.10.cloned.1.call-update) | async-done | bytes 1179664 | tf_op jit(solution)/shard_map/all_gather | solution.py:64
  149.7 27.9 %all-to-all-done = bf16[3,2,256,768]{2,1,0,3:T(2,128)(2,1)S(1)} async-done(((bf16[3,2,256,768]{2,1,0,3:T(2,128)(2,1)}), bf16[3,2,256,768]{2,1,0,3:T(2,128)(2,1)S(1)}, u32[]{:S(2)}, u32[]{:S(2)}) %all-to-all-start) | async-done | bytes 2359328 | tf_op jit(solution)/shard_map/all_to_all | solution.py:98
  183.4 29.9 %while.51 = (s32[]{:T(128)}, bf16[2,1024,192]{2,1,0:T(8,128)(2,1)}, f32[2,2,3,512]{3,2,1,0:T(4,128)S(1)}, bf16[2,1024,192]{1,2,0:T(8,128)(2,1)}, bf16[2,1024,192...) while((s32[]{:T(128)}, bf16[2,1024,192]{2,1,0:T(8,128)(2,1)}, ...), condition=%wide.region_5.6_spmd, body=%wide.region_0.5_spmd.sunk | while | flops 421625344 | bytes 26176296 | solution.py:137
  186.4 10.9 while.54
  201.4 10.9 while.54
  220.4 26.8 %all-gather = bf16[8,1,384]{2,1,0:T(2,128)(2,1)S(1)} all-gather(bf16[1,1,384]{2,1,0:T(2,128)(2,1)S(1)} %reshape.301), channel_id=1, replica_groups=mesh['dp'=8,'seq'=4] {'dp'}, dimensions={0}, use_global_device_ids=true | all-gather | bytes 6912 | tf_op jit(solution)/shard_map/all_gather | solution.py:72
  261.3 20.9 %multiply_convert_fusion.1 = (bf16[512,3072]{1,0:T(8,128)(2,1)}, f32[512,3072]{1,0:T(8,128)}, f32[512,3072]{1,0:T(8,128)}) fusion(f32[3072]{0:T(1024)S(1)} %bitcast.268, bf16[768,3072]{1,0:T(8,128)(2,1)} %all-gather.16.cloned.1.call-done, f32[512,768]{1,0:T(8,128)} %copy-done.21, f32[768]{0:T(1024)S(1)} %convert_element_type.180, ...), kind=kOutput, calls=%fused_computation.66 | convolution fusion | flops 2521694208 | bytes 22042624 | tf_op jit(solution)/shard_map/dot_general | solution.py:23
  282.2 59.2 %all-gather.18.cloned.1.call-done = bf16[3072,768]{1,0:T(8,128)(2,1)} async-done(((bf16[384,768]{1,0:T(8,128)(2,1)}), bf16[3072,768]{1,0:T(8,128)(2,1)}) %all-gather.18.cloned.1.call-update) | async-done | bytes 4718608 | tf_op jit(solution)/shard_map/all_gather | solution.py:68
  374.1 11.6 all-to-all-done.2
  385.9 70.7 %while.53 = (s32[]{:T(128)}, bf16[2,3,1024,192]{2,3,1,0:T(8,128)(2,1)}, bf16[2,1024,192]{1,2,0:T(8,128)(2,1)}, bf16[2,1024,192]{1,2,0:T(8,128)(2,1)S(1)}, f32[2,...) while((s32[]{:T(128)}, ...), condition=%wide.region_18.19_spmd, body=%wide.region_14.18_spmd.sunk | while | flops 1035337216 | bytes 144484816 | solution.py:252
  389.2 27.8 %while.55 = (s32[]{:T(128)}, f32[1024,3,64]{0,2,1:T(8,128)}, f32[1024,3,64]{0,2,1:T(8,128)}, bf16[2,512,192]{1,2,0:T(8,128)(2,1)}, bf16[2,512,3,64]{1,3,2,0:T(8,...) while((s32[]{:T(128)}, f32[1024,3,64]{0,2,1:T(8,128)}, ...), condition=%wide.region_17.17_spmd.clone, body=%wide.region_15.16_spmd.clone.sunk | while | flops 1031405056 | bytes 115951104 | solution.py:239
  424.4 27.8 %while.55 = (s32[]{:T(128)}, f32[1024,3,64]{0,2,1:T(8,128)}, f32[1024,3,64]{0,2,1:T(8,128)}, bf16[2,512,192]{1,2,0:T(8,128)(2,1)}, bf16[2,512,3,64]{1,3,2,0:T(8,...) while((s32[]{:T(128)}, f32[1024,3,64]{0,2,1:T(8,128)}, ...), condition=%wide.region_17.17_spmd.clone, body=%wide.region_15.16_spmd.clone.sunk | while | flops 1031405056 | bytes 115951104 | solution.py:239
  464.1 40.3 %all_to_all.66 = bf16[2,3,1024,192]{3,0,1,2:T(2,128)(2,1)} all-to-all(bf16[2,3,1024,192]{3,0,1,2:T(2,128)(2,1)S(1)} %copy.120), channel_id=1, replica_groups=mesh['dp'=8,'seq'=4] {'seq'}, dimensions={2} | all-to-all | bytes 4718592 | tf_op jit(solution)/shard_map/all_to_all | solution.py:256
  504.3 9.0 copy.129
  564.0 28.1 %reduce-scatter.19.cloned.1.call-done = f32[96,768]{1,0:T(8,128)} async-done(((f32[768,768]{1,0:T(8,128)}), f32[96,768]{1,0:T(8,128)}) %reduce-scatter.19.cloned.1.call-update) | async-done | bytes 294928
  594.0 69.7 %reduce-scatter.21.cloned.1.call-done = f32[96,768]{1,0:T(8,128)} async-done(((f32[768,768]{1,0:T(8,128)}), f32[96,768]{1,0:T(8,128)}) %reduce-scatter.21.cloned.1.call-update) | async-done | bytes 294928
  665.6 69.7 %reduce-scatter.23.cloned.1.call-done = f32[96,768]{1,0:T(8,128)} async-done(((f32[768,768]{1,0:T(8,128)}), f32[96,768]{1,0:T(8,128)}) %reduce-scatter.23.cloned.1.call-update) | async-done | bytes 294928
  737.2 69.5 %reduce-scatter.13.cloned.1.call-done = f32[96,768]{1,0:T(8,128)} async-done(((f32[768,768]{1,0:T(8,128)}), f32[96,768]{1,0:T(8,128)}) %reduce-scatter.13.cloned.1.call-update) | async-done | bytes 294928 | tf_op jit(solution)/shard_map/reduce_scatter | solution.py:276
  806.8 166.1 %reduce-scatter.15.cloned.1.call-done = f32[96,3072]{1,0:T(8,128)} async-done(((f32[768,3072]{1,0:T(8,128)}), f32[96,3072]{1,0:T(8,128)}) %reduce-scatter.15.cloned.1.call-update) | async-done | bytes 1179664 | tf_op jit(solution)/shard_map/reduce_scatter | solution.py:277
  972.9 166.0 %reduce-scatter.17.cloned.1.call-done = f32[384,768]{1,0:T(8,128)} async-done(((f32[3072,768]{1,0:T(8,128)}), f32[384,768]{1,0:T(8,128)}) %reduce-scatter.17.cloned.1.call-update) | async-done | bytes 1179664 | tf_op jit(solution)/shard_map/reduce_scatter | solution.py:278
  1142.0 35.7 %all-reduce.17 = (f32[768]{0:T(1024)S(1)}, f32[768]{0:T(1024)S(1)}, f32[768]{0:T(1024)S(1)}, f32[3072]{0:T(1024)S(1)}, f32[768]{0:T(1024)S(1)}, /*index=5*/f32[7...) all-reduce(f32[768]{0:T(1024)S(1)} %get-tuple-element.403, ...), channel_id=8, replica_groups=mesh['dp'=8,'seq'=4] {'dp'}, use_global_device_ids=true, to_apply=%region_32.33.clone | all-reduce | flops 9216 | bytes 73728
  1191.2 31.0 %all-reduce.23.cloned.1.call-done = (f32[96,768]{0,1:T(8,128)}, f32[96,768]{0,1:T(8,128)}, f32[96,768]{0,1:T(8,128)}, f32[96,768]{1,0:T(8,128)}, f32[96,3072]{1,0:T(8,128)}, /*index=5*/f32[384,768]{1,0:T(8,128)}) async-done(((f32[96,768]{0,1:T(8,128)}, f32[96,768]{0,1:T(8,128)}, f32[96,768]{0,1:T(8,128)}, f32[96,768]{1,0:T(8,128)}, f32[96,3072]{1,0:T(8,128)}, /*index=5*/f32[384,768]{1,0:T(8,128)}), ...) | async-done | bytes 3538960 | tf_op jit(solution)/shard_map/psum | solution.py:289
  (473 shorter events, 275.2 us)
Async XLA Ops:
  7.2 52.0 %all-gather.8.cloned.1.call-start = ((), (), s32[]{:S(2)}) async-start(), calls=%async_computation.10 | async-start | bytes 1327104 | tf_op jit(solution)/shard_map/all_gather | solution.py:63
  7.9 88.4 %all-gather.12.cloned.1.call-start = ((), (), s32[]{:S(2)}) async-start(), calls=%async_computation.12 | async-start | bytes 1327104 | tf_op jit(solution)/shard_map/all_gather | solution.py:65
  8.7 129.7 %all-gather.10.cloned.1.call-start = ((), (), s32[]{:S(2)}) async-start(), calls=%async_computation.11 | async-start | bytes 1327104 | tf_op jit(solution)/shard_map/all_gather | solution.py:64
  9.4 240.4 %all-gather.14.cloned.1.call-start = ((), (), s32[]{:S(2)}) async-start(), calls=%async_computation.13 | async-start | bytes 1327104 | tf_op jit(solution)/shard_map/all_gather | solution.py:66
  10.0 251.3 %all-gather.16.cloned.1.call-start = ((), (), s32[]{:S(2)}) async-start(), calls=%async_computation.14 | async-start | bytes 5308416 | tf_op jit(solution)/shard_map/all_gather | solution.py:67
  145.4 32.1 %all-to-all-start = ((bf16[3,2,256,768]{2,1,0,3:T(2,128)(2,1)}), bf16[3,2,256,768]{2,1,0,3:T(2,128)(2,1)S(1)}, u32[]{:S(2)}, u32[]{:S(2)}) async-start(bf16[3,2,256,768]{2,1,0,3:T(2,128)(2,1)} %pad_maximum_fusion), calls=%async_computation | async-start | bytes 4718592 | tf_op jit(solution)/shard_map/all_to_all | solution.py:98
  149.1 192.3 %all-gather.18.cloned.1.call-start = ((), (), s32[]{:S(2)}) async-start(), calls=%async_computation.15 | async-start | bytes 5308416 | tf_op jit(solution)/shard_map/all_gather | solution.py:68
  216.7 31.3 %all-to-all-start.1 = ((bf16[2,1024,192]{2,0,1:T(2,128)(2,1)}), bf16[2,1024,192]{2,0,1:T(2,128)(2,1)S(1)}, u32[]{:S(2)}, u32[]{:S(2)}) async-start(bf16[2,1024,192]{2,0,1:T(2,128)(2,1)} %copy.115), calls=%async_computation.1 | async-start | bytes 2097152 | tf_op jit(solution)/shard_map/all_to_all | solution.py:140
  220.4 144.1 %copy-start.41 = (f32[768]{0:T(1024)}, f32[768]{0:T(1024)S(1)}, u32[]{:S(2)}) copy-start(f32[768]{0:T(1024)S(1)} %convert_element_type.179) | copy-start | bytes 9220
  370.5 15.1 %all-to-all-start.2 = ((bf16[2,256,768]{1,0,2:T(2,128)(2,1)}), bf16[2,256,768]{1,0,2:T(2,128)(2,1)S(1)}, u32[]{:S(2)}, u32[]{:S(2)}) async-start(bf16[2,256,768]{1,0,2:T(2,128)(2,1)} %copy.117), calls=%async_computation.2 | async-start | bytes 1572864 | tf_op jit(solution)/shard_map/all_to_all | solution.py:183
  374.0 218.1 %reduce-scatter.19.cloned.1.call-start = ((), (), s32[]{:S(2)}) async-start(), calls=%async_computation.19 | async-start | bytes 2654208
  525.7 138.0 %reduce-scatter.21.cloned.1.call-start = ((), (), s32[]{:S(2)}) async-start(), calls=%async_computation.20 | async-start | bytes 2654208
  534.4 200.9 %reduce-scatter.23.cloned.1.call-start = ((), (), s32[]{:S(2)}) async-start(), calls=%async_computation.21 | async-start | bytes 2654208
  542.7 264.1 %reduce-scatter.13.cloned.1.call-start = ((), (), s32[]{:S(2)}) async-start(), calls=%async_computation.16 | async-start | bytes 2654208 | tf_op jit(solution)/shard_map/reduce_scatter | solution.py:276
  546.4 426.5 %reduce-scatter.15.cloned.1.call-start = ((), (), s32[]{:S(2)}) async-start(), calls=%async_computation.17 | async-start | bytes 10616832 | tf_op jit(solution)/shard_map/reduce_scatter | solution.py:277
  555.4 583.5 %reduce-scatter.17.cloned.1.call-start = ((), (), s32[]{:S(2)}) async-start(), calls=%async_computation.18 | async-start | bytes 10616832 | tf_op jit(solution)/shard_map/reduce_scatter | solution.py:278
  563.9 576.3 %copy-start.46 = (f32[2,256]{1,0:T(2,128)S(1)}, f32[2,256]{1,0:T(2,128)}, u32[]{:S(2)}) copy-start(f32[2,256]{1,0:T(2,128)} %get-tuple-element.530) | copy-start | bytes 6148
  564.0 658.2 %all-reduce.23.cloned.1.call-start = ((), (), s32[]{:S(2)}) async-start(), calls=%async_computation.22 | async-start | bytes 7667712 | tf_op jit(solution)/shard_map/psum | solution.py:289
  737.2 404.7 %copy-start.38 = (f32[768]{0:T(1024)S(1)}, f32[768]{0:T(1024)}, u32[]{:S(2)}) copy-start(f32[768]{0:T(1024)} %get-tuple-element.400) | copy-start | bytes 9220
  737.2 404.7 %copy-start.39 = (f32[768]{0:T(1024)S(1)}, f32[768]{0:T(1024)}, u32[]{:S(2)}) copy-start(f32[768]{0:T(1024)} %get-tuple-element.501) | copy-start | bytes 9220
  737.2 404.7 %copy-start.40 = (f32[768]{0:T(1024)S(1)}, f32[768]{0:T(1024)}, u32[]{:S(2)}) copy-start(f32[768]{0:T(1024)} %get-tuple-element.505) | copy-start | bytes 9220
  737.2 404.7 %copy-start.43 = (f32[3072]{0:T(1024)S(1)}, f32[3072]{0:T(1024)}, u32[]{:S(2)}) copy-start(f32[3072]{0:T(1024)} %get-tuple-element.503) | copy-start | bytes 36868
  737.2 404.7 %copy-start.49 = (f32[768]{0:T(1024)S(1)}, f32[768]{0:T(1024)}, u32[]{:S(2)}) copy-start(f32[768]{0:T(1024)} %get-tuple-element.398) | copy-start | bytes 9220
  737.2 404.7 %copy-start.50 = (f32[768]{0:T(1024)S(1)}, f32[768]{0:T(1024)}, u32[]{:S(2)}) copy-start(f32[768]{0:T(1024)} %get-tuple-element.404) | copy-start | bytes 9220
  (99 other events, 991.2 us)
Sparse Core Ops, SparseCore 0:
  10.2 43.9 all-gather.7
  56.4 39.8 all-gather.11
  98.5 39.8 all-gather.9
  140.4 39.8 all-gather.13
  182.4 78.8 all-gather.15
  263.3 78.0 all-gather.17
  525.8 66.2 reduce-scatter.18
  595.6 68.0 reduce-scatter.20
  667.2 68.0 reduce-scatter.22
  738.7 68.0 reduce-scatter.12
  810.4 162.4 reduce-scatter.14
  976.3 162.5 reduce-scatter.16
  1142.3 79.8 all-reduce.22
where the time goes:
time: 1250 us; the launch traced here: 1240 us
  waiting for transfers between devices  784 us (63%)
  blocking collectives  149 us (12%)
  matrix products  141 us (11%)
  local copies, waits for them, and re-layouts  98.8 us (8%)
  other arithmetic  36 us (3%)
  between operations  16.9 us (1%)
    unnamed x16, waiting for transfers between devices  171 us
    reduce_scatter x1, waiting for transfers between devices, local(): lax.psum_scatter(up_weight_grad, 'dp', scatter_dimension=0, tiled=True)  166 us
    reduce_scatter x1, waiting for transfers between devices, local(): lax.psum_scatter(down_weight_grad, 'dp', scatter_dimension=0, tiled=True)  166 us
    unnamed x2, blocking collectives  75.6 us
    reduce_scatter x1, waiting for transfers between devices, local(): lax.psum_scatter(output_weight_grad, 'dp', scatter_dimension=0, tiled=True)  69.5 us
    all_gather x1, waiting for transfers between devices, local(): lax.all_gather(down_weight, 'dp', axis=0, tiled=True)  59.2 us
    all_to_all x1, blocking collectives, local(): lax.all_to_all(head_grads, 'seq', split_axis=2, concat_axis=3, tiled=True)  40.3 us
    all_gather x1, waiting for transfers between devices, local(): lax.all_gather(key_weight, 'dp', axis=0, tiled=True)  39.3 us
  transfers between devices with their start and end apart: 16, of which 13 were waited for; matrix products, arithmetic and copies ran while one was open for 11% of the time, Pallas kernels for 0%

commit v1 on v0

--- a/solution.py
+++ b/solution.py
@@ -6,6 +6,35 @@
 HEAD_DIM = 64
 eps_norm = 1e-05
 masked_score = -1000000000.0
+
+
+def classes_pack(xin, row_dim):
+    xin = jnp.moveaxis(xin, 0, row_dim)
+    outer = xin.shape
+    return xin.reshape(*outer[:row_dim], outer[row_dim] * outer[row_dim + 1], *outer[row_dim + 2 :])
+
+
+def _name_trails(base_x, lane_axis, on_dim):
+    n_parts = lax.axis_size(lane_axis)
+    frames = [(b, (b + 1) % n_parts) for b in range(n_parts)]
+    sides = [(at, rr) for rr, at in frames]
+    v1, right_arr = ([], [])
+    for ix in range(n_parts - 1):
+        if ix % 2 == 0:
+            earlier = lax.ppermute(v1[-1] if v1 else base_x, perm=frames, axis_name=lane_axis)
+            v1.append(earlier)
+        else:
+            right_arr.append(
+                lax.ppermute(
+                    right_arr[-1] if right_arr else base_x, axis_name=lane_axis, perm=sides
+                )
+            )
+    all_values = jnp.stack([*v1[::-1], base_x, *right_arr], axis=0)
+    k_now = lax.axis_index(lane_axis)
+    even = len(v1)
+    block_next = k_now - even
+    all_values = all_values[(jnp.arange(n_parts) - block_next) % n_parts]
+    return classes_pack(all_values, on_dim)
 
 
 def layer_norm(hidden, gain_vec, shift_vec):
@@ -62,7 +91,7 @@
     gathered = (
         lax.all_gather(query_weight, "dp", axis=0, tiled=True),
         lax.all_gather(key_weight, "dp", axis=0, tiled=True),
-        lax.all_gather(value_weight, "dp", axis=0, tiled=True),
+        _name_trails(value_weight, "dp", 0),
         lax.all_gather(output_weight, "dp", axis=0, tiled=True),
         lax.all_gather(up_weight, "dp", axis=0, tiled=True),
         lax.all_gather(down_weight, "dp", axis=0, tiled=True),

time: 1250 us -> 1250 us (level)
  waiting for transfers between devices: 784 us -> 762 us
  starting transfers between devices: 11.7 us -> 26.1 us
  local copies, waits for them, and re-layouts: 98.8 us -> 113 us
    all_gather x1, waiting for transfers between devices: 39.3 us -> 0.05 us  [local(): lax.all_gather(key_weight, 'dp', axis=0, tiled=True)]
    psum x1, waiting for transfers between devices: 31 us -> 68.1 us  [local(): lax.psum((summed[0], summed[1], summed[2], summed[3], summed[4], summed[5...]
    all_gather x1, waiting for transfers between devices: 34.2 us -> 0.01 us  [local(): lax.all_gather(value_weight, 'dp', axis=0, tiled=True)]
    ppermute x0 -> x7, waiting for transfers between devices: none -> 24.4 us  [the longest x4 16.3 us: _name_trails(): lax.ppermute(v1[-1] if v1 else base_x, perm=frames, axis_name=lane_axis)]
    ppermute x0 -> x7, starting transfers between devices: none -> 13.7 us  [the longest x3 9.23 us: _name_trails(): lax.ppermute(right_arr[-1] if right_arr else base_x, axis_name=lane_axis,...]
    unnamed x131 -> x136, local copies, waits for them, and re-layouts: 36.7 us -> 38.6 us
  transfers between devices with their start and end apart: 16 -> 23, of which waited for: 13 -> 14; matrix products, arithmetic and copies ran while one was open for 11% -> 12% of each run, Pallas kernels for 0% -> 0%
where the time goes in v1:
time: 1250 us
  waiting for transfers between devices  762 us (61%)
  blocking collectives  146 us (12%)
  matrix products  146 us (12%)
  local copies, waits for them, and re-layouts  113 us (9%)
  other arithmetic  36.4 us (3%)
  starting transfers between devices  26.1 us (2%)
  between operations  16.9 us (1%)
    unnamed x16, waiting for transfers between devices  170 us
    reduce_scatter x1, waiting for transfers between devices, local(): lax.psum_scatter(up_weight_grad, 'dp', scatter_dimension=0, tiled=True)  166 us
    reduce_scatter x1, waiting for transfers between devices, local(): lax.psum_scatter(down_weight_grad, 'dp', scatter_dimension=0, tiled=True)  166 us
    unnamed x2, blocking collectives  73.1 us
    reduce_scatter x1, waiting for transfers between devices, local(): lax.psum_scatter(output_weight_grad, 'dp', scatter_dimension=0, tiled=True)  69.9 us
    psum x1, waiting for transfers between devices, local(): lax.psum((summed[0], summed[1], summed[2], summed[3], summed[4], summed[5...  68.1 us
    all_gather x1, waiting for transfers between devices, local(): lax.all_gather(down_weight, 'dp', axis=0, tiled=True)  57.1 us
    all_to_all x1, blocking collectives, local(): lax.all_to_all(head_grads, 'seq', split_axis=2, concat_axis=3, tiled=True)  40.3 us
  transfers between devices with their start and end apart: 23, of which 14 were waited for; matrix products, arithmetic and copies ran while one was open for 12% of the time, Pallas kernels for 0%

profile of v1, /device:TPU:0, one launch (start us, length us, event | category | flops | bytes accessed | tf_op | source)
XLA Modules:
  0.0 1247.1 jit_solution(6676058342330993932)
XLA Ops:
  48.7 37.1 %all-reduce.20 = (bf16[768]{0:T(1024)(128)(2,1)S(1)}, bf16[768]{0:T(1024)(128)(2,1)S(1)}, bf16[768]{0:T(1024)(128)(2,1)}, bf16[768]{0:T(1024)(128)(2,1)}, bf16[7...) all-reduce(bf16[768]{0:T(1024)(128)(2,1)S(1)} %dynamic-update-slice, ...), channel_id=1, replica_groups=mesh['dp'=8,'seq'=4] {'dp'}, use_global_device_ids=true, to_apply=%add.1 | all-reduce | flops 6144 | bytes 24576
  112.9 27.9 %all-to-all-done = bf16[3,2,256,768]{2,1,0,3:T(2,128)(2,1)S(1)} async-done(((bf16[3,2,256,768]{2,1,0,3:T(2,128)(2,1)}), bf16[3,2,256,768]{2,1,0,3:T(2,128)(2,1)S(1)}, u32[]{:S(2)}, u32[]{:S(2)}) %all-to-all-start) | async-done | bytes 2359328 | tf_op jit(solution)/shard_map/all_to_all | solution.py:127
  147.0 33.4 %while.51 = (s32[]{:T(128)}, bf16[2,1024,192]{2,1,0:T(8,128)(2,1)}, f32[2,2,3,512]{3,2,1,0:T(4,128)}, bf16[2,1024,192]{1,2,0:T(8,128)(2,1)S(1)}, bf16[2,1024,192...) while((s32[]{:T(128)}, bf16[2,1024,192]{2,1,0:T(8,128)(2,1)}, ...), condition=%wide.region_5.6_spmd, body=%wide.region_0.5_spmd.sunk | while | flops 421625344 | bytes 27946360 | solution.py:166
  148.8 12.3 while.54
  165.4 12.3 while.54
  188.4 26.4 %all-gather = bf16[8,1,384]{2,1,0:T(2,128)(2,1)S(1)} all-gather(bf16[1,1,384]{2,1,0:T(2,128)(2,1)S(1)} %reshape.362), channel_id=1, replica_groups=mesh['dp'=8,'seq'=4] {'dp'}, dimensions={0}, use_global_device_ids=true | all-gather | bytes 6912 | tf_op jit(solution)/shard_map/all_gather | solution.py:101
  227.8 20.8 %multiply_convert_fusion.1 = (bf16[512,3072]{1,0:T(8,128)(2,1)}, f32[512,3072]{1,0:T(8,128)}, f32[512,3072]{1,0:T(8,128)}) fusion(f32[3072]{0:T(1024)S(1)} %bitcast.289, bf16[768,3072]{1,0:T(8,128)(2,1)} %all-gather.14.cloned.1.call-done, f32[512,768]{1,0:T(8,128)} %copy-done.24, f32[768]{0:T(1024)S(1)} %convert_element_type.184, ...), kind=kOutput, calls=%fused_computation.67 | convolution fusion | flops 2521694208 | bytes 22042624 | tf_op jit(solution)/shard_map/dot_general | solution.py:52
  248.6 57.1 %all-gather.16.cloned.1.call-done = bf16[3072,768]{1,0:T(8,128)(2,1)} async-done(((bf16[384,768]{1,0:T(8,128)(2,1)}), bf16[3072,768]{1,0:T(8,128)(2,1)}) %all-gather.16.cloned.1.call-update) | async-done | bytes 4718608 | tf_op jit(solution)/shard_map/all_gather | solution.py:97
  316.5 9.0 convert_reduce_fusion
  338.2 11.6 all-to-all-done.2
  350.9 71.7 %while.53 = (s32[]{:T(128)}, bf16[2,3,1024,192]{2,3,1,0:T(8,128)(2,1)}, bf16[2,1024,192]{1,2,0:T(8,128)(2,1)S(1)}, bf16[2,1024,192]{1,2,0:T(8,128)(2,1)}, f32[2,...) while((s32[]{:T(128)}, ...), condition=%wide.region_18.19_spmd, body=%wide.region_14.18_spmd.sunk | while | flops 1035337216 | bytes 150579664 | solution.py:281
  354.5 27.9 %while.55 = (s32[]{:T(128)}, f32[1024,3,64]{0,2,1:T(8,128)}, f32[1024,3,64]{0,2,1:T(8,128)}, bf16[2,512,192]{1,2,0:T(8,128)(2,1)}, bf16[2,512,3,64]{1,3,2,0:T(8,...) while((s32[]{:T(128)}, f32[1024,3,64]{0,2,1:T(8,128)}, ...), condition=%wide.region_17.17_spmd.clone, body=%wide.region_15.16_spmd.clone.sunk | while | flops 1031405056 | bytes 115951104 | solution.py:268
  390.3 27.9 %while.55 = (s32[]{:T(128)}, f32[1024,3,64]{0,2,1:T(8,128)}, f32[1024,3,64]{0,2,1:T(8,128)}, bf16[2,512,192]{1,2,0:T(8,128)(2,1)}, bf16[2,512,3,64]{1,3,2,0:T(8,...) while((s32[]{:T(128)}, f32[1024,3,64]{0,2,1:T(8,128)}, ...), condition=%wide.region_17.17_spmd.clone, body=%wide.region_15.16_spmd.clone.sunk | while | flops 1031405056 | bytes 115951104 | solution.py:268
  430.1 40.3 %all_to_all.66 = bf16[2,3,1024,192]{3,0,1,2:T(2,128)(2,1)} all-to-all(bf16[2,3,1024,192]{3,0,1,2:T(2,128)(2,1)S(1)} %copy.120), channel_id=1, replica_groups=mesh['dp'=8,'seq'=4] {'seq'}, dimensions={2} | all-to-all | bytes 4718592 | tf_op jit(solution)/shard_map/all_to_all | solution.py:285
  470.4 9.1 copy.129
  521.6 9.0 fusion.64
  531.2 27.1 %reduce-scatter.19.cloned.1.call-done = f32[96,768]{1,0:T(8,128)} async-done(((f32[768,768]{1,0:T(8,128)}), f32[96,768]{1,0:T(8,128)}) %reduce-scatter.19.cloned.1.call-update) | async-done | bytes 294928
  560.2 69.8 %reduce-scatter.21.cloned.1.call-done = f32[96,768]{1,0:T(8,128)} async-done(((f32[768,768]{1,0:T(8,128)}), f32[96,768]{1,0:T(8,128)}) %reduce-scatter.21.cloned.1.call-update) | async-done | bytes 294928
  631.9 69.9 %reduce-scatter.23.cloned.1.call-done = f32[96,768]{1,0:T(8,128)} async-done(((f32[768,768]{1,0:T(8,128)}), f32[96,768]{1,0:T(8,128)}) %reduce-scatter.23.cloned.1.call-update) | async-done | bytes 294928
  703.6 69.9 %reduce-scatter.13.cloned.1.call-done = f32[96,768]{1,0:T(8,128)} async-done(((f32[768,768]{1,0:T(8,128)}), f32[96,768]{1,0:T(8,128)}) %reduce-scatter.13.cloned.1.call-update) | async-done | bytes 294928 | tf_op jit(solution)/shard_map/reduce_scatter | solution.py:305
  773.5 166.0 %reduce-scatter.17.cloned.1.call-done = f32[384,768]{1,0:T(8,128)} async-done(((f32[3072,768]{1,0:T(8,128)}), f32[384,768]{1,0:T(8,128)}) %reduce-scatter.17.cloned.1.call-update) | async-done | bytes 1179664 | tf_op jit(solution)/shard_map/reduce_scatter | solution.py:307
  939.5 166.2 %reduce-scatter.15.cloned.1.call-done = f32[96,3072]{1,0:T(8,128)} async-done(((f32[768,3072]{1,0:T(8,128)}), f32[96,3072]{1,0:T(8,128)}) %reduce-scatter.15.cloned.1.call-update) | async-done | bytes 1179664 | tf_op jit(solution)/shard_map/reduce_scatter | solution.py:306
  1108.8 36.1 %all-reduce.17 = (f32[768]{0:T(1024)S(1)}, f32[768]{0:T(1024)S(1)}, f32[768]{0:T(1024)S(1)}, f32[3072]{0:T(1024)S(1)}, f32[768]{0:T(1024)S(1)}, /*index=5*/f32[7...) all-reduce(f32[768]{0:T(1024)S(1)} %get-tuple-element.403, ...), channel_id=8, replica_groups=mesh['dp'=8,'seq'=4] {'dp'}, use_global_device_ids=true, to_apply=%region_32.33.clone | all-reduce | flops 9216 | bytes 73728
  1162.8 68.1 %all-reduce.23.cloned.1.call-done = (f32[96,768]{0,1:T(8,128)}, f32[96,768]{0,1:T(8,128)}, f32[96,768]{0,1:T(8,128)}, f32[96,768]{1,0:T(8,128)}, f32[96,3072]{1,0:T(8,128)}, /*index=5*/f32[384,768]{1,0:T(8,128)}) async-done(((f32[96,768]{0,1:T(8,128)}, f32[96,768]{0,1:T(8,128)}, f32[96,768]{0,1:T(8,128)}, f32[96,768]{1,0:T(8,128)}, f32[96,3072]{1,0:T(8,128)}, /*index=5*/f32[384,768]{1,0:T(8,128)}), ...) | async-done | bytes 3538960 | tf_op jit(solution)/shard_map/psum | solution.py:318
  (512 shorter events, 307.9 us)
Async XLA Ops:
  7.2 91.5 %all-gather.8.cloned.1.call-start = ((), (), s32[]{:S(2)}) async-start(), calls=%async_computation.10 | async-start | bytes 1327104 | tf_op jit(solution)/shard_map/all_gather | solution.py:92
  7.9 93.6 %all-gather.10.cloned.1.call-start = ((), (), s32[]{:S(2)}) async-start(), calls=%async_computation.11 | async-start | bytes 1327104 | tf_op jit(solution)/shard_map/all_gather | solution.py:93
  8.7 215.2 %all-gather.12.cloned.1.call-start = ((), (), s32[]{:S(2)}) async-start(), calls=%async_computation.12 | async-start | bytes 1327104 | tf_op jit(solution)/shard_map/all_gather | solution.py:95
  9.4 218.4 %all-gather.14.cloned.1.call-start = ((), (), s32[]{:S(2)}) async-start(), calls=%async_computation.13 | async-start | bytes 5308416 | tf_op jit(solution)/shard_map/all_gather | solution.py:96
  10.0 10.1 collective-permute-start
  20.1 10.7 collective-permute-start.1
  20.1 10.9 collective-permute-start.4
  30.8 8.0 collective-permute-start.2
  31.0 54.7 %collective-permute-start.5 = (bf16[96,768]{1,0:T(8,128)(2,1)S(1)}, bf16[96,768]{1,0:T(8,128)(2,1)S(1)}, u32[]{:S(2)}, u32[]{:S(2)}) collective-permute-start(bf16[96,768]{1,0:T(8,128)(2,1)S(1)} %collective-permute-done.4), channel_id=1, source_target_pairs={{4,0},{8,4},{12,8},{16,12},{20,16},{24,20},{28,24},{0,28},{5,1},{9... | collective-permute-start | bytes 442376 | tf_op jit(solution)/shard_map/ppermute | solution.py:28
  38.8 47.1 %collective-permute-start.3 = (bf16[96,768]{1,0:T(8,128)(2,1)S(1)}, bf16[96,768]{1,0:T(8,128)(2,1)S(1)}, u32[]{:S(2)}, u32[]{:S(2)}) collective-permute-start(bf16[96,768]{1,0:T(8,128)(2,1)S(1)} %collective-permute-done.2), channel_id=1, source_target_pairs={{0,4},{4,8},{8,12},{12,16},{16,20},{20,24},{24,28},{28,0},{1,5},{5... | collective-permute-start | bytes 442376 | tf_op jit(solution)/shard_map/ppermute | solution.py:24
  85.8 8.3 collective-permute-start.6
  108.6 32.1 %all-to-all-start = ((bf16[3,2,256,768]{2,1,0,3:T(2,128)(2,1)}), bf16[3,2,256,768]{2,1,0,3:T(2,128)(2,1)S(1)}, u32[]{:S(2)}, u32[]{:S(2)}) async-start(bf16[3,2,256,768]{2,1,0,3:T(2,128)(2,1)} %pad_maximum_fusion), calls=%async_computation | async-start | bytes 4718592 | tf_op jit(solution)/shard_map/all_to_all | solution.py:127
  112.2 193.5 %all-gather.16.cloned.1.call-start = ((), (), s32[]{:S(2)}) async-start(), calls=%async_computation.14 | async-start | bytes 5308416 | tf_op jit(solution)/shard_map/all_gather | solution.py:97
  183.9 31.6 %all-to-all-start.1 = ((bf16[2,1024,192]{2,0,1:T(2,128)(2,1)}), bf16[2,1024,192]{2,0,1:T(2,128)(2,1)}, u32[]{:S(2)}, u32[]{:S(2)}) async-start(bf16[2,1024,192]{2,0,1:T(2,128)(2,1)} %copy.115), calls=%async_computation.1 | async-start | bytes 2097152 | tf_op jit(solution)/shard_map/all_to_all | solution.py:169
  334.6 15.1 %all-to-all-start.2 = ((bf16[2,256,768]{1,0,2:T(2,128)(2,1)}), bf16[2,256,768]{1,0,2:T(2,128)(2,1)S(1)}, u32[]{:S(2)}, u32[]{:S(2)}) async-start(bf16[2,256,768]{1,0,2:T(2,128)(2,1)} %copy.117), calls=%async_computation.2 | async-start | bytes 1572864 | tf_op jit(solution)/shard_map/all_to_all | solution.py:212
  338.1 220.1 %reduce-scatter.19.cloned.1.call-start = ((), (), s32[]{:S(2)}) async-start(), calls=%async_computation.19 | async-start | bytes 2654208
  491.7 138.2 %reduce-scatter.21.cloned.1.call-start = ((), (), s32[]{:S(2)}) async-start(), calls=%async_computation.20 | async-start | bytes 2654208
  500.6 201.1 %reduce-scatter.23.cloned.1.call-start = ((), (), s32[]{:S(2)}) async-start(), calls=%async_computation.21 | async-start | bytes 2654208
  508.7 264.7 %reduce-scatter.13.cloned.1.call-start = ((), (), s32[]{:S(2)}) async-start(), calls=%async_computation.16 | async-start | bytes 2654208 | tf_op jit(solution)/shard_map/reduce_scatter | solution.py:305
  512.4 427.1 %reduce-scatter.17.cloned.1.call-start = ((), (), s32[]{:S(2)}) async-start(), calls=%async_computation.18 | async-start | bytes 10616832 | tf_op jit(solution)/shard_map/reduce_scatter | solution.py:307
  520.9 584.8 %reduce-scatter.15.cloned.1.call-start = ((), (), s32[]{:S(2)}) async-start(), calls=%async_computation.17 | async-start | bytes 10616832 | tf_op jit(solution)/shard_map/reduce_scatter | solution.py:306
  530.6 628.3 %all-gather.18.cloned.1.call-start = ((), (), s32[]{:S(2)}) async-start(), calls=%async_computation.15 | async-start | bytes 1327104 | tf_op jit(solution)/shard_map/all_gather | solution.py:183
  531.1 699.7 %all-reduce.23.cloned.1.call-start = ((), (), s32[]{:S(2)}) async-start(), calls=%async_computation.22 | async-start | bytes 7667712 | tf_op jit(solution)/shard_map/psum | solution.py:318
  631.9 475.2 %copy-start.48 = (f32[2,256]{1,0:T(2,128)S(1)}, f32[2,256]{1,0:T(2,128)}, u32[]{:S(2)}) copy-start(f32[2,256]{1,0:T(2,128)} %get-tuple-element.530) | copy-start | bytes 6148
  (113 other events, 1071.0 us)
Sparse Core Ops, SparseCore 0:
  10.2 48.4 all-gather.7
  60.9 40.5 all-gather.9
  103.7 40.9 all-gather.11
  146.7 78.8 all-gather.13
  227.7 78.0 all-gather.15
  491.9 66.3 reduce-scatter.18
  561.8 68.1 reduce-scatter.20
  633.5 68.1 reduce-scatter.22
  705.2 68.2 reduce-scatter.12
  776.9 162.5 reduce-scatter.16
  943.1 162.5 reduce-scatter.14
  1107.7 40.3 all-gather.17
  1151.5 79.3 all-reduce.22
